TPU v7x, 256 devices: a whole 4x4x8 slice. The times are simulated.
256 devices in a mesh: gx: 8 (over y, core), gy: 4 (over z_lo), gz: 8 (over z_hi, x).
Axes of the slice: x: 4, y: 4, z: 8 (z_hi: 2, z_lo: 4; z = z_hi * 4 + z_lo), core: 2. Of those that a mesh axis runs over, the one named last changes fastest.
Arguments:
- tokens: bfloat16 [2048, 8192], P(('gx', 'gy'), 'gz'), may hold values from -6 to 6
- gate_weight: bfloat16 [8192, 28672], P('gz', ('gx', 'gy')), may hold values from -0.0625 to 0.0625
- up_weight: bfloat16 [8192, 28672], P('gz', ('gx', 'gy')), may hold values from -0.0625 to 0.0625
- down_weight: bfloat16 [28672, 8192], P(('gx', 'gy'), 'gz'), may hold values from -0.03125 to 0.03125
Outputs:
- layer_output: bfloat16 [2048, 8192], P(('gx', 'gy'), 'gz')
All inputs are finite; a program needn't handle non-finite values.
Results may differ from a plain program's by a relative error of at most 0.029.
Values may be sent and summed in bfloat16 or wider, within the bound.
A program may use at most 128 MiB of HBM per device.

v0:
```python
import jax
import jax.numpy as jnp
from jax import lax
from jax.sharding import PartitionSpec as P


def shards(tokens, gate_weight, up_weight, down_weight):
    gathered = lax.all_gather(tokens, "gx", axis=0, tiled=True)

    def column_product(weight_piece):
        return jnp.dot(gathered, weight_piece, preferred_element_type=jnp.float32)

    gate_partial = column_product(lax.all_gather(gate_weight, "gy", axis=1, tiled=True))
    up_partial = column_product(lax.all_gather(up_weight, "gy", axis=1, tiled=True))
    gate_sum, up_sum = (
        lax.psum_scatter(
            gate_partial.astype(jnp.bfloat16), "gz", scatter_dimension=0, tiled=True
        ).astype(jnp.float32),
        lax.psum_scatter(
            up_partial.astype(jnp.bfloat16), "gz", scatter_dimension=0, tiled=True
        ).astype(jnp.float32),
    )
    local_hidden = (jax.nn.silu(gate_sum) * up_sum).astype(jnp.bfloat16)
    hidden = lax.all_gather(local_hidden, "gz", axis=0, tiled=True)
    down_partial = jnp.dot(
        hidden,
        lax.all_gather(down_weight, "gy", axis=0, tiled=True),
        preferred_element_type=jnp.float32,
    )
    layer_output = lax.psum_scatter(
        down_partial.astype(jnp.bfloat16), "gx", scatter_dimension=0, tiled=True
    )
    return layer_output


def solution(mesh):
    return jax.shard_map(
        shards,
        mesh=mesh,
        in_specs=(
            P(("gx", "gy"), "gz"),
            P("gz", ("gx", "gy")),
            P("gz", ("gx", "gy")),
            P(("gx", "gy"), "gz"),
        ),
        out_specs=P(("gx", "gy"), "gz"),
        check_vma=False,
    )
```

profile of v0, /device:TPU:2, one launch (start us, length us, event | category | flops | bytes accessed | tf_op | source)
XLA Modules:
  0.0 839.3 jit_solution(120754620333667691)
XLA Ops:
  6.5 0.0 all-gather.6.cloned.1.call-start
  6.5 0.7 all-gather.6.cloned.1.call-update
  7.3 0.0 all-gather.8.cloned.1.call-start
  7.3 0.7 all-gather.8.cloned.1.call-update
  8.0 0.0 all-gather.10.cloned.1.call-start
  8.1 0.7 all-gather.10.cloned.1.call-update
  8.7 0.0 reduce-scatter.4.cloned.1.call-start
  8.8 29.3 %all-gather.6.cloned.1.call-done = bf16[512,1024]{1,0:T(8,128)(2,1)} async-done(((bf16[64,1024]{1,0:T(8,128)(2,1)}), bf16[512,1024]{1,0:T(8,128)(2,1)}) %all-gather.6.cloned.1.call-update) | async-done | bytes 1048592 | tf_op jit(solution)/shard_map/all_gather | solution.py:8
  38.1 0.0 copy-start
  38.1 137.6 %all-gather.8.cloned.1.call-done = bf16[1024,3584]{1,0:T(8,128)(2,1)} async-done(((bf16[1024,896]{1,0:T(8,128)(2,1)}), bf16[1024,3584]{1,0:T(8,128)(2,1)}) %all-gather.8.cloned.1.call-update) | async-done | bytes 7340048 | tf_op jit(solution)/shard_map/all_gather | solution.py:13
  175.7 9.2 %convolution_convert_fusion.1 = bf16[512,3584]{1,0:T(8,128)(2,1)} fusion(bf16[512,1024]{1,0:T(8,128)(2,1)} %all-gather.6.cloned.1.call-done, bf16[1024,3584]{1,0:T(8,128)(2,1)} %all-gather.8.cloned.1.call-done), kind=kOutput, calls=%fused_computation.1 | convolution fusion | flops 3759931392 | bytes 12058624 | tf_op jit(solution)/shard_map/dot_general | solution.py:11
  184.9 0.0 reduce-scatter.4.cloned.1.call-update
  184.9 0.0 reduce-scatter.6.cloned.1.call-start
  185.0 128.1 %all-gather.10.cloned.1.call-done = bf16[1024,3584]{1,0:T(8,128)(2,1)} async-done(((bf16[1024,896]{1,0:T(8,128)(2,1)}), bf16[1024,3584]{1,0:T(8,128)(2,1)}) %all-gather.10.cloned.1.call-update) | async-done | bytes 7340048 | tf_op jit(solution)/shard_map/all_gather | solution.py:14
  313.1 0.0 copy-done
  313.1 8.4 %convolution_convert_fusion = bf16[512,3584]{1,0:T(8,128)(2,1)} fusion(bf16[512,1024]{1,0:T(8,128)(2,1)S(1)} %copy-done, bf16[1024,3584]{1,0:T(8,128)(2,1)} %all-gather.10.cloned.1.call-done), kind=kOutput, calls=%fused_computation | convolution fusion | flops 3759931392 | bytes 12058624 | tf_op jit(solution)/shard_map/dot_general | solution.py:11
  321.5 0.0 reduce-scatter.6.cloned.1.call-update
  321.6 0.0 all-gather.14.cloned.1.call-start
  321.6 0.5 all-gather.14.cloned.1.call-update
  322.1 0.0 all-gather.12.cloned.1.call-start
  322.2 115.4 %reduce-scatter.4.cloned.1.call-done = bf16[64,3584]{1,0:T(8,128)(2,1)} async-done(((bf16[512,3584]{1,0:T(8,128)(2,1)}), bf16[64,3584]{1,0:T(8,128)(2,1)}) %reduce-scatter.4.cloned.1.call-update) | async-done | bytes 458768 | tf_op jit(solution)/shard_map/reduce_scatter | solution.py:16
  437.6 121.3 %reduce-scatter.6.cloned.1.call-done = bf16[64,3584]{1,0:T(8,128)(2,1)} async-done(((bf16[512,3584]{1,0:T(8,128)(2,1)}), bf16[64,3584]{1,0:T(8,128)(2,1)}) %reduce-scatter.6.cloned.1.call-update) | async-done | bytes 458768 | tf_op jit(solution)/shard_map/reduce_scatter | solution.py:19
  558.9 2.2 fusion.4
  561.1 0.0 all-gather.12.cloned.1.call-update
  561.1 0.0 reduce-scatter.8.cloned.1.call-start
  561.2 131.1 %all-gather.14.cloned.1.call-done = bf16[3584,1024]{1,0:T(8,128)(2,1)} async-done(((bf16[896,1024]{1,0:T(8,128)(2,1)}), bf16[3584,1024]{1,0:T(8,128)(2,1)}) %all-gather.14.cloned.1.call-update) | async-done | bytes 7340048 | tf_op jit(solution)/shard_map/all_gather | solution.py:27
  692.3 100.6 %all-gather.12.cloned.1.call-done = bf16[512,3584]{1,0:T(8,128)(2,1)} async-done(((bf16[64,3584]{1,0:T(8,128)(2,1)}), bf16[512,3584]{1,0:T(8,128)(2,1)}) %all-gather.12.cloned.1.call-update) | async-done | bytes 3670032 | tf_op jit(solution)/shard_map/all_gather | solution.py:24
  792.9 9.1 %convolution_convert_fusion.2 = bf16[512,1024]{1,0:T(8,128)(2,1)} fusion(bf16[512,3584]{1,0:T(8,128)(2,1)} %all-gather.12.cloned.1.call-done, bf16[3584,1024]{1,0:T(8,128)(2,1)} %all-gather.14.cloned.1.call-done), kind=kOutput, calls=%fused_computation.2 | convolution fusion | flops 3758620672 | bytes 12058624 | tf_op jit(solution)/shard_map/dot_general | solution.py:25
  802.0 0.0 reduce-scatter.8.cloned.1.call-update
  802.0 30.5 %reduce-scatter.8.cloned.1.call-done = bf16[64,1024]{1,0:T(8,128)(2,1)} async-done(((bf16[512,1024]{1,0:T(8,128)(2,1)}), bf16[64,1024]{1,0:T(8,128)(2,1)}) %reduce-scatter.8.cloned.1.call-update) | async-done | bytes 131088 | tf_op jit(solution)/shard_map/reduce_scatter | solution.py:30
Async XLA Ops:
  6.5 31.6 %all-gather.6.cloned.1.call-start = ((), (), s32[]{:S(2)}) async-start(), calls=%async_computation.3 | async-start | bytes 1179648 | tf_op jit(solution)/shard_map/all_gather | solution.py:8
  7.3 168.4 %all-gather.8.cloned.1.call-start = ((), (), s32[]{:S(2)}) async-start(), calls=%async_computation.4 | async-start | bytes 9175040 | tf_op jit(solution)/shard_map/all_gather | solution.py:13
  8.0 305.1 %all-gather.10.cloned.1.call-start = ((), (), s32[]{:S(2)}) async-start(), calls=%async_computation.6 | async-start | bytes 9175040 | tf_op jit(solution)/shard_map/all_gather | solution.py:14
  8.7 428.9 %reduce-scatter.4.cloned.1.call-start = ((), (), s32[]{:S(2)}) async-start(), calls=%async_computation.5 | async-start | bytes 4128768 | tf_op jit(solution)/shard_map/reduce_scatter | solution.py:16
  38.1 275.0 %copy-start = (bf16[512,1024]{1,0:T(8,128)(2,1)S(1)}, bf16[512,1024]{1,0:T(8,128)(2,1)}, u32[]{:S(2)}) copy-start(bf16[512,1024]{1,0:T(8,128)(2,1)} %all-gather.6.cloned.1.call-done) | copy-start | bytes 3145732
  184.9 374.0 %reduce-scatter.6.cloned.1.call-start = ((), (), s32[]{:S(2)}) async-start(), calls=%async_computation.7 | async-start | bytes 4128768 | tf_op jit(solution)/shard_map/reduce_scatter | solution.py:19
  321.6 370.7 %all-gather.14.cloned.1.call-start = ((), (), s32[]{:S(2)}) async-start(), calls=%async_computation.9 | async-start | bytes 9175040 | tf_op jit(solution)/shard_map/all_gather | solution.py:27
  322.1 470.7 %all-gather.12.cloned.1.call-start = ((), (), s32[]{:S(2)}) async-start(), calls=%async_computation.8 | async-start | bytes 4128768 | tf_op jit(solution)/shard_map/all_gather | solution.py:24
  561.1 271.4 %reduce-scatter.8.cloned.1.call-start = ((), (), s32[]{:S(2)}) async-start(), calls=%async_computation.10 | async-start | bytes 1179648 | tf_op jit(solution)/shard_map/reduce_scatter | solution.py:30
Sparse Core Ops, SparseCore 0:
  9.2 28.8 all-gather.5
  40.0 135.6 all-gather.7
  177.5 135.5 all-gather.9
  317.2 120.3 reduce-scatter.3
  442.3 116.5 reduce-scatter.5
  560.6 131.6 all-gather.13
  694.9 97.9 all-gather.11
  802.1 30.3 reduce-scatter.7
where the time goes:
time: 839 us
  waiting for transfers between devices  797 us (95%)
  matrix products  26.8 us (3%)
  between operations  13.5 us (2%)
    all_gather x1, waiting for transfers between devices, shards(): lax.all_gather(gate_weight, 'gy', axis=1, tiled=True)  138 us
    all_gather x1, waiting for transfers between devices, shards(): lax.all_gather(down_weight, 'gy', axis=0, tiled=True)  131 us
    all_gather x1, waiting for transfers between devices, shards(): lax.all_gather(up_weight, 'gy', axis=1, tiled=True)  128 us
    reduce_scatter x1, waiting for transfers between devices, shards(): lax.psum_scatter(up_partial.astype(jnp.bfloat16), 'gz', scatter_dimension...  121 us
    reduce_scatter x1, waiting for transfers between devices, shards(): lax.psum_scatter(gate_partial.astype(jnp.bfloat16), 'gz', scatter_dimensi...  115 us
    all_gather x1, waiting for transfers between devices, shards(): hidden = lax.all_gather(local_hidden, 'gz', axis=0, tiled=True)  101 us
    reduce_scatter x1, waiting for transfers between devices, shards(): lax.psum_scatter(down_partial.astype(jnp.bfloat16), 'gx', scatter_dimensi...  30.5 us
    all_gather x1, waiting for transfers between devices, shards(): gathered = lax.all_gather(tokens, 'gx', axis=0, tiled=True)  29.3 us
  transfers between devices with their start and end apart: 8, of which 8 were waited for; matrix products, arithmetic and copies ran while one was open for 2% of the time, Pallas kernels for 0%

commit v1 on v0

--- a/solution.py
+++ b/solution.py
@@ -4,8 +4,16 @@
 from jax.sharding import PartitionSpec as P
 
 
+def gather_from_all(value, axis, dim):
+    length = lax.axis_size(axis)
+    repeats = [length if d == dim else 1 for d in range(value.ndim)]
+    return lax.all_to_all(
+        jnp.tile(value, repeats), axis, split_axis=dim, concat_axis=dim, tiled=True
+    )
+
+
 def shards(tokens, gate_weight, up_weight, down_weight):
-    gathered = lax.all_gather(tokens, "gx", axis=0, tiled=True)
+    gathered = gather_from_all(tokens, "gx", 0)
 
     def column_product(weight_piece):
         return jnp.dot(gathered, weight_piece, preferred_element_type=jnp.float32)

time: 839 us -> 810 us (0.965)
  waiting for transfers between devices: 797 us -> 746 us
  blocking collectives: 0 us -> 20.4 us
    all_gather x1 -> x0, waiting for transfers between devices: 29.3 us -> none  [shards(): gathered = lax.all_gather(tokens, 'gx', axis=0, tiled=True)]
    all_to_all x0 -> x1, blocking collectives: none -> 20.4 us  [gather_from_all(): lax.all_to_all(jnp.tile(value, repeats), axis, split_axis=dim, concat_axi...]
    all_gather x1, waiting for transfers between devices: 138 us -> 119 us  [shards(): lax.all_gather(gate_weight, 'gy', axis=1, tiled=True)]
  transfers between devices with their start and end apart: 8 -> 7, of which waited for: 8 -> 7; matrix products, arithmetic and copies ran while one was open for 2% -> 2% of each run, Pallas kernels for 0% -> 0%
where the time goes in v1:
time: 810 us
  waiting for transfers between devices  746 us (92%)
  matrix products  26.1 us (3%)
  blocking collectives  20.4 us (3%)
  between operations  13.5 us (2%)
    all_gather x1, waiting for transfers between devices, shards(): lax.all_gather(down_weight, 'gy', axis=0, tiled=True)  131 us
    all_gather x1, waiting for transfers between devices, shards(): lax.all_gather(up_weight, 'gy', axis=1, tiled=True)  129 us
    reduce_scatter x1, waiting for transfers between devices, shards(): lax.psum_scatter(up_partial.astype(jnp.bfloat16), 'gz', scatter_dimension...  119 us
    all_gather x1, waiting for transfers between devices, shards(): lax.all_gather(gate_weight, 'gy', axis=1, tiled=True)  119 us
    reduce_scatter x1, waiting for transfers between devices, shards(): lax.psum_scatter(gate_partial.astype(jnp.bfloat16), 'gz', scatter_dimensi...  116 us
    all_gather x1, waiting for transfers between devices, shards(): hidden = lax.all_gather(local_hidden, 'gz', axis=0, tiled=True)  100 us
    reduce_scatter x1, waiting for transfers between devices, shards(): lax.psum_scatter(down_partial.astype(jnp.bfloat16), 'gx', scatter_dimensi...  30.5 us
    all_to_all x1, blocking collectives, gather_from_all(): lax.all_to_all(jnp.tile(value, repeats), axis, split_axis=dim, concat_axi...  20.4 us
  transfers between devices with their start and end apart: 7, of which 7 were waited for; matrix products, arithmetic and copies ran while one was open for 2% of the time, Pallas kernels for 0%

profile of v1, /device:TPU:2, one launch (start us, length us, event | category | flops | bytes accessed | tf_op | source)
XLA Modules:
  0.0 809.8 jit_solution(7448881920751002648)
XLA Ops:
  6.5 0.0 all-gather.5.cloned.1.call-start
  6.5 0.7 all-gather.5.cloned.1.call-update
  7.3 0.0 all-gather.7.cloned.1.call-start
  7.3 0.7 all-gather.7.cloned.1.call-update
  8.0 0.0 reduce-scatter.4.cloned.1.call-start
  8.1 1.0 tile.2
  9.1 20.4 %all_to_all.9 = bf16[8,64,1024]{2,1,0:T(8,128)(2,1)S(1)} all-to-all(bf16[8,64,1024]{2,1,0:T(8,128)(2,1)S(1)} %tile.2), channel_id=1, replica_groups=mesh['gx'=8,'gy'=4,'gz'=8] {'gx'}, dimensions={0} | all-to-all | bytes 2097152 | tf_op jit(solution)/shard_map/all_to_all | solution.py:10
  29.4 118.5 %all-gather.5.cloned.1.call-done = bf16[1024,3584]{1,0:T(8,128)(2,1)} async-done(((bf16[1024,896]{1,0:T(8,128)(2,1)}), bf16[1024,3584]{1,0:T(8,128)(2,1)}) %all-gather.5.cloned.1.call-update) | async-done | bytes 7340048 | tf_op jit(solution)/shard_map/all_gather | solution.py:21
  148.0 8.5 %convolution_convert_fusion.1 = bf16[512,3584]{1,0:T(8,128)(2,1)} fusion(bf16[512,1024]{1,0:T(8,128)(2,1)S(1)} %bitcast.7, bf16[1024,3584]{1,0:T(8,128)(2,1)} %all-gather.5.cloned.1.call-done), kind=kOutput, calls=%fused_computation.1 | convolution fusion | flops 3759931392 | bytes 12058624 | tf_op jit(solution)/shard_map/dot_general | solution.py:19
  156.5 0.0 reduce-scatter.4.cloned.1.call-update
  156.5 0.0 reduce-scatter.6.cloned.1.call-start
  156.6 128.8 %all-gather.7.cloned.1.call-done = bf16[1024,3584]{1,0:T(8,128)(2,1)} async-done(((bf16[1024,896]{1,0:T(8,128)(2,1)}), bf16[1024,3584]{1,0:T(8,128)(2,1)}) %all-gather.7.cloned.1.call-update) | async-done | bytes 7340048 | tf_op jit(solution)/shard_map/all_gather | solution.py:22
  285.4 8.5 %convolution_convert_fusion = bf16[512,3584]{1,0:T(8,128)(2,1)} fusion(bf16[512,1024]{1,0:T(8,128)(2,1)S(1)} %bitcast.8, bf16[1024,3584]{1,0:T(8,128)(2,1)} %all-gather.7.cloned.1.call-done), kind=kOutput, calls=%fused_computation | convolution fusion | flops 3759931392 | bytes 12058624 | tf_op jit(solution)/shard_map/dot_general | solution.py:19
  293.8 0.0 reduce-scatter.6.cloned.1.call-update
  293.9 0.0 all-gather.11.cloned.1.call-start
  293.9 0.5 all-gather.11.cloned.1.call-update
  294.5 0.0 all-gather.9.cloned.1.call-start
  294.5 115.6 %reduce-scatter.4.cloned.1.call-done = bf16[64,3584]{1,0:T(8,128)(2,1)} async-done(((bf16[512,3584]{1,0:T(8,128)(2,1)}), bf16[64,3584]{1,0:T(8,128)(2,1)}) %reduce-scatter.4.cloned.1.call-update) | async-done | bytes 458768 | tf_op jit(solution)/shard_map/reduce_scatter | solution.py:24
  410.1 119.4 %reduce-scatter.6.cloned.1.call-done = bf16[64,3584]{1,0:T(8,128)(2,1)} async-done(((bf16[512,3584]{1,0:T(8,128)(2,1)}), bf16[64,3584]{1,0:T(8,128)(2,1)}) %reduce-scatter.6.cloned.1.call-update) | async-done | bytes 458768 | tf_op jit(solution)/shard_map/reduce_scatter | solution.py:27
  529.5 2.2 fusion.4
  531.7 0.0 all-gather.9.cloned.1.call-update
  531.7 0.0 reduce-scatter.8.cloned.1.call-start
  531.8 131.0 %all-gather.11.cloned.1.call-done = bf16[3584,1024]{1,0:T(8,128)(2,1)} async-done(((bf16[896,1024]{1,0:T(8,128)(2,1)}), bf16[3584,1024]{1,0:T(8,128)(2,1)}) %all-gather.11.cloned.1.call-update) | async-done | bytes 7340048 | tf_op jit(solution)/shard_map/all_gather | solution.py:35
  662.8 100.5 %all-gather.9.cloned.1.call-done = bf16[512,3584]{1,0:T(8,128)(2,1)} async-done(((bf16[64,3584]{1,0:T(8,128)(2,1)}), bf16[512,3584]{1,0:T(8,128)(2,1)}) %all-gather.9.cloned.1.call-update) | async-done | bytes 3670032 | tf_op jit(solution)/shard_map/all_gather | solution.py:32
  763.3 9.1 %convolution_convert_fusion.2 = bf16[512,1024]{1,0:T(8,128)(2,1)} fusion(bf16[512,3584]{1,0:T(8,128)(2,1)} %all-gather.9.cloned.1.call-done, bf16[3584,1024]{1,0:T(8,128)(2,1)} %all-gather.11.cloned.1.call-done), kind=kOutput, calls=%fused_computation.2 | convolution fusion | flops 3758620672 | bytes 12058624 | tf_op jit(solution)/shard_map/dot_general | solution.py:33
  772.4 0.0 reduce-scatter.8.cloned.1.call-update
  772.4 30.5 %reduce-scatter.8.cloned.1.call-done = bf16[64,1024]{1,0:T(8,128)(2,1)} async-done(((bf16[512,1024]{1,0:T(8,128)(2,1)}), bf16[64,1024]{1,0:T(8,128)(2,1)}) %reduce-scatter.8.cloned.1.call-update) | async-done | bytes 131088 | tf_op jit(solution)/shard_map/reduce_scatter | solution.py:38
Async XLA Ops:
  6.5 141.5 %all-gather.5.cloned.1.call-start = ((), (), s32[]{:S(2)}) async-start(), calls=%async_computation.4 | async-start | bytes 9175040 | tf_op jit(solution)/shard_map/all_gather | solution.py:21
  7.3 278.1 %all-gather.7.cloned.1.call-start = ((), (), s32[]{:S(2)}) async-start(), calls=%async_computation.6 | async-start | bytes 9175040 | tf_op jit(solution)/shard_map/all_gather | solution.py:22
  8.0 402.1 %reduce-scatter.4.cloned.1.call-start = ((), (), s32[]{:S(2)}) async-start(), calls=%async_computation.5 | async-start | bytes 4128768 | tf_op jit(solution)/shard_map/reduce_scatter | solution.py:24
  156.5 373.0 %reduce-scatter.6.cloned.1.call-start = ((), (), s32[]{:S(2)}) async-start(), calls=%async_computation.7 | async-start | bytes 4128768 | tf_op jit(solution)/shard_map/reduce_scatter | solution.py:27
  293.9 369.0 %all-gather.11.cloned.1.call-start = ((), (), s32[]{:S(2)}) async-start(), calls=%async_computation.9 | async-start | bytes 9175040 | tf_op jit(solution)/shard_map/all_gather | solution.py:35
  294.5 468.8 %all-gather.9.cloned.1.call-start = ((), (), s32[]{:S(2)}) async-start(), calls=%async_computation.8 | async-start | bytes 4128768 | tf_op jit(solution)/shard_map/all_gather | solution.py:32
  531.7 271.2 %reduce-scatter.8.cloned.1.call-start = ((), (), s32[]{:S(2)}) async-start(), calls=%async_computation.10 | async-start | bytes 1179648 | tf_op jit(solution)/shard_map/reduce_scatter | solution.py:38
Sparse Core Ops, SparseCore 0:
  9.2 138.7 all-gather.4
  149.8 135.5 all-gather.6
  289.6 120.4 reduce-scatter.3
  414.8 114.6 reduce-scatter.5
  531.1 131.6 all-gather.10
  665.3 97.9 all-gather.8
  772.6 30.3 reduce-scatter.7
